TPU v7x, 512 devices: a whole 4x4x16 slice. The times are simulated.
512 devices in a mesh: leaf: 64 (over y, z_lo, core), grp: 8 (over z_hi, x).
Axes of the slice: x: 4, y: 4, z: 16 (z_hi: 2, z_lo: 8; z = z_hi * 8 + z_lo), core: 2. Of those that a mesh axis runs over, the one named last changes fastest.
Arguments:
- slot_parent: int32 [512], P(('leaf', 'grp')), may hold values from -1 to 7, as said below
- leaf_matrix: float32 [512, 384, 384], P(('leaf', 'grp')), as said below
- coupling: float32 [512, 384, 128], P(('leaf', 'grp')), may hold values from -0.3125 to 0.3125
- leaf_residual_rows: float32 [512, 384], P(('leaf', 'grp')), may hold values from -6 to 6
- node_matrix: float32 [64, 128, 128], P('grp', 'leaf'), as said below
- node_link: float32 [64, 128, 128], P('grp', 'leaf'), may hold values from -0.5 to 0.5
- node_rhs: float32 [64, 128], P('grp', 'leaf'), may hold values from -6 to 6
- root_matrix: float32 [128, 128], replicated, as said below
- root_rhs: float32 [128], replicated, may hold values from -6 to 6
Outputs:
- leaf_dir: float32 [512, 384], P(('leaf', 'grp'))
- node_dir: float32 [64, 128], P('grp', 'leaf')
- root_dir: float32 [128], replicated
Inputs may be any that keep to these rules, and one draw needn't show every extreme that they name: `slot_parent`: -1 marks an empty slot; otherwise the value is the section-2 node, among the 8 nodes of the slot's grp index, to which the leaf belongs. On every device the live slots come first; a device may hold no live slot or only live slots. `leaf_matrix`: each block is symmetric positive definite with smallest eigenvalue at least 0.1. `node_matrix`: each block is symmetric positive definite with smallest eigenvalue at least 0.1. `root_matrix`: symmetric positive definite with smallest eigenvalue at least 0.1.
All inputs are finite; a program needn't handle non-finite values.
Results may differ from a plain program's by a relative error of at most 0.00018.
Values sent between devices are 32-bit elements; how exact they have to be, the bound alone decides.
A program may use at most 64 MiB of HBM per device.

v0:
```python
import jax
import jax.numpy as jnp
from jax import lax
from jax.sharding import PartitionSpec as P

highest = lax.Precision.HIGHEST


def lower_solve(factor, values):
    return lax.linalg.triangular_solve(factor, values, left_side=True, lower=True)


def upper_solve(factor, values):
    return lax.linalg.triangular_solve(factor, values, left_side=True, lower=True, transpose_a=True)


def solve_root(root_matrix, root_rhs, root_part, root_shift):
    root_fac = jnp.linalg.cholesky(root_matrix + root_part)
    root_vec = root_rhs - root_shift
    return upper_solve(root_fac, lower_solve(root_fac, root_vec[:, None]))[:, 0]


def body(
    slot_parent,
    leaf_matrix,
    coupling,
    leaf_residual_rows,
    node_matrix,
    node_link,
    node_rhs,
    root_matrix,
    root_rhs,
):
    groups = node_matrix.shape[0]
    row_band = node_matrix.shape[1]
    active = slot_parent >= 0
    active_mask = active.astype(jnp.float32)
    leaf_fac = jnp.linalg.cholesky(leaf_matrix)
    solved = lower_solve(leaf_fac, coupling)
    reduced = lower_solve(leaf_fac, leaf_residual_rows[:, :, None])[:, :, 0]
    onehot = (slot_parent[:, None] == jnp.arange(groups, dtype=jnp.int32)[None, :]).astype(
        jnp.float32
    )
    gram = jnp.einsum("sab,sac->sbc", solved, solved, precision=highest)
    projected = jnp.einsum("sab,sa->sb", solved, reduced, precision=highest)
    partial_schur = jnp.einsum("sk,sbc->kbc", onehot, gram, precision=highest)
    partial_vec = jnp.einsum("sk,sb->kb", onehot, projected, precision=highest)
    zero_index = jnp.zeros((), jnp.int32)
    offset = lax.axis_index("leaf") * row_band
    placed = lax.dynamic_update_slice(
        jnp.zeros_like(partial_schur), node_matrix, (zero_index, offset, zero_index)
    )
    placed_rhs = lax.dynamic_update_slice(
        jnp.zeros_like(partial_vec), node_rhs, (zero_index, offset)
    )
    partial_schur = partial_schur + placed
    partial_vec = partial_vec - placed_rhs
    schur, node_vec = lax.psum((partial_schur, partial_vec), "leaf")
    links = lax.all_gather(node_link, "leaf", axis=1, tiled=True)
    node_fac = jnp.linalg.cholesky(schur)
    link_solved = lower_solve(node_fac, links)
    vec_solved = lower_solve(node_fac, node_vec[:, :, None])[:, :, 0]
    root_part = jnp.einsum("kar,kas->rs", link_solved, link_solved, precision=highest)
    root_shift = jnp.einsum("kar,ka->r", link_solved, vec_solved, precision=highest)
    root_part, root_shift = lax.psum((root_part, root_shift), "grp")
    root_dir = solve_root(root_matrix, root_rhs, root_part, root_shift)
    moved = vec_solved + jnp.einsum("kar,r->ka", link_solved, root_dir, precision=highest)
    directions = upper_solve(node_fac, moved[:, :, None])[:, :, 0]
    node_dir = lax.dynamic_slice_in_dim(directions, offset, row_band, 1)
    parent_dir = jnp.einsum("sk,kb->sb", onehot, directions, precision=highest)
    correction = reduced - jnp.einsum("sab,sb->sa", solved, parent_dir, precision=highest)
    leaf_dir = upper_solve(leaf_fac, correction[:, :, None])[:, :, 0] * active_mask[:, None]
    return (leaf_dir, node_dir, root_dir)


def solution(mesh):
    return jax.shard_map(
        body,
        mesh=mesh,
        in_specs=(
            P(("leaf", "grp")),
            P(("leaf", "grp"), None, None),
            P(("leaf", "grp"), None, None),
            P(("leaf", "grp"), None),
            P("grp", "leaf", None),
            P("grp", "leaf", None),
            P("grp", "leaf"),
            P(),
            P(),
        ),
        out_specs=(P(("leaf", "grp"), None), P("grp", "leaf"), P()),
        check_vma=False,
    )
```

profile of v0, /device:TPU:1, one launch (start us, length us, event | category | flops | bytes accessed | tf_op | source)
XLA Modules:
  0.0 1306.3 jit_solution(7474695091724387954)
XLA Ops:
  7.2 1.4 copy.32
  8.7 11.7 custom-call.48
  20.4 9.8 custom-call.49
  30.9 11.7 custom-call.50
  42.6 10.0 custom-call.51
  53.1 11.7 custom-call.52
  64.8 0.7 compare_reduce_fusion.2
  68.3 6.0 while.1
  68.9 1.4 bitcast_dynamic-update-slice_fusion.2
  70.9 1.4 bitcast_dynamic-update-slice_fusion.2
  72.9 1.4 bitcast_dynamic-update-slice_fusion.2
  74.3 29.5 %custom-call.53 = f32[1,3,128,128]{2,3,1,0:T(8,128)S(1)} custom-call(f32[1,3,128,128]{3,2,1,0:T(8,128)S(1)} %bitcast.321), custom_call_target="InvertDiagBlocksLowerTriangular" | custom-call | tf_op jit(solution)/shard_map/triangular_solve | solution.py:14
  106.3 0.7 copy-done.5
  107.5 2.6 add.88
  110.1 0.8 copy-done
  112.9 0.7 copy-done.9
  114.2 422.5 %psum.29 = f32[8,128]{0,1:T(8,128)S(1)} all-reduce(f32[8,128]{0,1:T(8,128)S(1)} %multiply_subtract_fusion), channel_id=1, replica_groups=mesh['leaf'=64,'grp'=8] {'leaf'}, use_global_device_ids=true, to_apply=%region_9.10 | all-reduce | flops 1024 | bytes 8192 | tf_op jit(solution)/shard_map/psum | solution.py:58
  536.8 0.8 copy-done.4
  537.8 125.2 %all_gather.3 = f32[8,128,128]{2,0,1:T(8,128)S(1)} all-gather(f32[8,2,128]{2,0,1:T(8,128)S(1)} %copy.36), channel_id=1, replica_groups=mesh['leaf'=64,'grp'=8] {'leaf'}, dimensions={1}, use_global_device_ids=true | all-gather | bytes 532480 | tf_op jit(solution)/shard_map/all_gather | solution.py:59
  663.0 286.3 %all-reduce.4.cloned.1.call-done = f32[8,128,128]{1,2,0:T(8,128)} async-done(((f32[8,128,128]{1,2,0:T(8,128)}), f32[8,128,128]{1,2,0:T(8,128)}) %all-reduce.4.cloned.1.call-update) | async-done | bytes 524304 | tf_op jit(solution)/shard_map/psum | solution.py:58
  949.3 1.3 copy.35
  950.7 93.8 %custom-call.54 = f32[8,128,128]{2,1,0:T(8,128)S(1)} custom-call(f32[8,128,128]{2,1,0:T(8,128)S(1)} %fusion.22), custom_call_target="Cholesky" | custom-call | tf_op jit(solution)/shard_map/jit(cholesky)/cholesky | solution.py:60
  1044.8 78.6 %custom-call.55 = f32[8,1,128,128]{2,3,1,0:T(8,128)S(1)} custom-call(f32[8,1,128,128]{3,2,1,0:T(8,128)S(1)} %select_bitcast_fusion), custom_call_target="InvertDiagBlocksLowerTriangular" | custom-call | tf_op jit(solution)/shard_map/triangular_solve | solution.py:14
  1123.4 1.0 fusion.18
  1124.9 1.6 convolution_bitcast_fusion.1
  1127.0 35.3 %psum.31 = f32[128]{0:T(128)S(1)} all-reduce(f32[128]{0:T(128)S(1)} %convolution_bitcast_fusion.18), channel_id=1, replica_groups=mesh['leaf'=64,'grp'=8] {'grp'}, use_global_device_ids=true, to_apply=%region_13.14 | all-reduce | flops 128 | bytes 1024 | tf_op jit(solution)/shard_map/psum | solution.py:65
  1162.3 108.2 %all-reduce.6.cloned.1.call-done = f32[128,128]{0,1:T(8,128)} async-done(((f32[128,128]{0,1:T(8,128)}), f32[128,128]{0,1:T(8,128)}) %all-reduce.6.cloned.1.call-update) | async-done | bytes 65552 | tf_op jit(solution)/shard_map/psum | solution.py:65
  1270.5 0.8 add.90
  1271.4 11.7 cholesky.287
  1283.8 0.7 fusion.28
  1284.5 9.8 custom-call.56
  1295.3 0.9 fusion.16
  (95 shorter events, 14.7 us)
Async XLA Ops:
  7.2 942.1 %all-reduce.4.cloned.1.call-start = ((), (), s32[]{:S(2)}) async-start(), calls=%async_computation | async-start | bytes 1048576 | tf_op jit(solution)/shard_map/psum | solution.py:58
  7.2 1.4 copy-start.1
  68.2 35.6 %copy-start.3 = (f32[1,384,128]{2,1,0:T(8,128)S(1)}, f32[1,384,128]{2,1,0:T(8,128)}, u32[]{:S(2)}) copy-start(f32[1,384,128]{2,1,0:T(8,128)} %param.11) | copy-start | bytes 589828
  106.3 0.7 copy-start.5
  110.1 0.8 copy-start
  111.0 0.7 copy-start.8
  111.0 1159.5 %all-reduce.6.cloned.1.call-start = ((), (), s32[]{:S(2)}) async-start(), calls=%async_computation.1 | async-start | bytes 131072 | tf_op jit(solution)/shard_map/psum | solution.py:65
  112.8 0.7 copy-start.9
  113.5 0.7 copy-start.6
  536.8 0.8 copy-start.4
  949.3 1.3 copy-start.2
  1284.5 9.8 copy-start.10
  1294.7 0.6 copy-start.7
Sparse Core Ops, SparseCore 0:
  111.1 838.1 all-reduce.3
  1126.7 143.7 all-reduce.5
where the time goes:
time: 1320 us; the launch traced here: 1310 us
  blocking collectives  583 us (44%)
  waiting for transfers between devices  395 us (30%)
  other arithmetic  284 us (22%)
  between operations  17.6 us (1%)
  local copies, waits for them, and re-layouts  16.6 us (1%)
    psum x1, blocking collectives, body(): schur, node_vec = lax.psum((partial_schur, partial_vec), 'leaf')  423 us
    psum x1, waiting for transfers between devices, body(): schur, node_vec = lax.psum((partial_schur, partial_vec), 'leaf')  286 us
    all_gather x1, blocking collectives, body(): links = lax.all_gather(node_link, 'leaf', axis=1, tiled=True)  125 us
    another operation x7, other arithmetic, upper_solve(): lax.linalg.triangular_solve(factor, values, left_side=True, lower=True, t...  119 us
    psum x1, waiting for transfers between devices, body(): root_part, root_shift = lax.psum((root_part, root_shift), 'grp')  108 us
    another operation x3, other arithmetic, body(): node_fac = jnp.linalg.cholesky(schur)  93.9 us
    another operation x12, other arithmetic, body(): leaf_fac = jnp.linalg.cholesky(leaf_matrix)  56.4 us
    psum x1, blocking collectives, body(): root_part, root_shift = lax.psum((root_part, root_shift), 'grp')  35.3 us
  transfers between devices with their start and end apart: 2, of which 2 were waited for; matrix products, arithmetic and copies ran while one was open for 0% of the time, Pallas kernels for 0%

commit v1 on v0

v1 whole, which is shorter than its diff:
```python
import jax
import jax.numpy as jnp
from jax import lax
from jax.experimental import pallas as pl
from jax.experimental.pallas import tpu as pltpu
from jax.sharding import PartitionSpec as P

f32 = jnp.float32
MESH = pl.DeviceIdType.MESH
HI = lax.Precision.HIGHEST
N = 128
AUG = 136


def dot(a, b):
    return jnp.dot(a, b, precision=HI, preferred_element_type=f32)


def dot_nt(a, b):
    return lax.dot_general(
        a, b, (((1,), (1,)), ((), ())), precision=HI, preferred_element_type=f32
    )


def lane_bcast(x, index):
    return jnp.take_along_axis(x, index, axis=1, mode="promise_in_bounds")


def row_bcast(row):
    return jnp.broadcast_to(row, (8, N))


def invert(d_ref, p_ref):
    lane = lax.broadcasted_iota(jnp.int32, (8, N), 1)
    sub = lax.broadcasted_iota(jnp.int32, (8, N), 0)
    groups = N // 8
    first = d_ref[0:8, :]
    for j in range(8):
        p_ref[8 * j : 8 * j + 8, :] = lane_bcast(first, jnp.full((8, N), j, jnp.int32))

    def block(k, carry):
        base = pl.multiple_of(k * 8, 8)
        base_next = pl.multiple_of(jnp.minimum(k + 1, groups - 1) * 8, 8)
        here = [jnp.full((8, N), base + j, jnp.int32) for j in range(8)]
        after = [jnp.full((8, N), base_next + j, jnp.int32) for j in range(8)]
        s = {}
        for j in range(8):
            for i in range(j + 1):
                s[i, j] = row_bcast(p_ref[8 * j + i : 8 * j + i + 1, :])
        r = [row_bcast(d_ref[pl.ds(base + j, 1), :]) for j in range(8)]
        d = [d_ref[g * 8 : (g + 1) * 8, :] for g in range(groups)]
        dn = d_ref[pl.ds(base_next, 8), :]
        c, cn = [], []
        for j in range(8):
            cn.append(lane_bcast(dn, here[j]))
            c.append([lane_bcast(d[g], here[j]) for g in range(groups)])
        inside = (lane >= base) & (lane < base + 8)
        r = [jnp.where(inside, jnp.where(lane == base + j, 1.0, 0.0), r[j]) for j in range(8)]
        low, inv = {}, []
        for j in range(8):
            inv.append(1.0 / s[j, j])
            for i in range(j + 1, 8):
                low[i, j] = s[j, i] * inv[j]
            for i in range(j + 1, 8):
                for m in range(i, 8):
                    s[i, m] = s[i, m] - low[i, j] * s[j, m]
            for i in range(j + 1, 8):
                r[i] = r[i] - low[i, j] * r[j]
        x = [r[j] * inv[j] for j in range(8)]
        for j in range(7, -1, -1):
            for i in range(j):
                x[i] = x[i] - low[j, i] * x[j]

        def update(rows, cols):
            kept = jnp.where(inside, 0.0, rows)
            t = [cols[j] * x[j] for j in range(8)]
            return kept - (((t[0] + t[1]) + (t[2] + t[3])) + ((t[4] + t[5]) + (t[6] + t[7])))

        upcoming = update(dn, cn)
        for j in range(8):
            p_ref[8 * j : 8 * j + 8, :] = lane_bcast(upcoming, after[j])
        for g in range(groups):
            d_ref[g * 8 : (g + 1) * 8, :] = update(d[g], [c[j][g] for j in range(8)])
        new = x[0]
        for j in range(1, 8):
            new = jnp.where(sub == j, x[j], new)
        d_ref[pl.ds(base, 8), :] = new
        return carry

    lax.fori_loop(0, groups, block, 0)


def kernel(
    parent, amat, coup, resid, nmat, nlink, nrhs, rmat, rrhs,
    leaf_out, node_out, root_out,
    bt, dinv, pbuf, e1, rem1, e2, rem2, h3, wts,
    ntile, gath, snd, recv_y, acc_o, recv_c, acc_m, recv_z,
    nsys, nlinks, naug, hmat, rparts, send_r, recv_r, part, recv_g, tot, recv_t,
    msg, recv_n, zt, nd8,
    s_n, r_n, s_y, r_y, s_c, r_c, s_z, r_z, s_r, r_r, s_g, r_g, s_t, r_t, s_m, r_m,
):
    me = lax.axis_index("leaf")
    grp = lax.axis_index("grp")
    y, z, core = me // 16, (me // 2) % 8, me % 2
    own_z = 4 - grp // 4
    owner = z == own_z
    mine = 2 * y + core

    def dev(leaf):
        return {"leaf": leaf, "grp": grp}

    def owner_leaf(m, oz):
        return (m // 2) * 16 + oz * 2 + m % 2

    barrier = pltpu.get_barrier_semaphore()

    def greet(t, carry):
        pl.semaphore_signal(barrier, inc=1, device_id=dev((me + t) % 64), device_id_type=MESH)
        return carry

    lax.fori_loop(1, 64, greet, 0)

    @pl.when(owner)
    def _():
        def greet_far(t, carry):
            g = (grp + t) % 8
            pl.semaphore_signal(
                barrier, inc=1,
                device_id={"leaf": owner_leaf(mine, 4 - g // 4), "grp": g}, device_id_type=MESH,
            )
            return carry

        lax.fori_loop(1, 8, greet_far, 0)

    sub = lax.broadcasted_iota(jnp.int32, (8, N), 0)
    lane = lax.broadcasted_iota(jnp.int32, (8, N), 1)
    wts[...] = jnp.where(sub == parent[0], 1.0, 0.0)
    for b in range(3):
        bt[0:N, b * N : (b + 1) * N] = coup[0, b * N : (b + 1) * N, :].T
        bt[N:AUG, b * N : (b + 1) * N] = jnp.where(
            sub == 0, row_bcast(resid[:, b * N : (b + 1) * N]), 0.0
        )
    nd8[...] = jnp.zeros((8, N), f32)
    nd8[:, 0:2] = nrhs[...]
    shifted = pltpu.roll(nd8[...], 2 * me, 1)
    for q in range(8):
        ntile[q, 0:2, :] = nmat[q]
        ntile[q, 2:4, :] = nlink[q]
        ntile[q, 4:8, :] = jnp.where(
            lax.broadcasted_iota(jnp.int32, (4, N), 0) == 0,
            jnp.broadcast_to(shifted[q : q + 1, :], (4, N)), 0.0
        )

    dinv[...] = amat[0, 0:N, 0:N]
    invert(dinv, pbuf)

    @pl.when(owner)
    def _():
        pl.semaphore_wait(barrier, 70)

    @pl.when(jnp.logical_not(owner))
    def _():
        pl.semaphore_wait(barrier, 63)

    def node_copy(q, target):
        return pltpu.make_async_remote_copy(
            src_ref=ntile.at[q], dst_ref=gath.at[me], send_sem=s_n.at[q], recv_sem=r_n,
            device_id=dev(target), device_id_type=MESH,
        )

    for q in range(8):
        target = owner_leaf(q, own_z)

        @pl.when(target != me)
        def _():
            node_copy(q, target).start()

        @pl.when(target == me)
        def _():
            gath[me] = ntile[q]

    d1 = dinv[...]
    e1[0:256, :] = dot(amat[0, N:384, 0:N], d1)
    e1[256:392, :] = dot(bt[:, 0:N], d1)
    snd[0:AUG, :] = dot_nt(e1[256:392, :], bt[0:N, 0:N])
    rem1[0:256, :] = amat[0, N:384, N:384] - dot(e1[0:256, :], amat[0, 0:N, N:384])
    rem1[256:392, :] = bt[:, N:384] - dot(e1[256:392, :], amat[0, 0:N, N:384])
    dinv[...] = rem1[0:N, 0:N]
    invert(dinv, pbuf)
    e2[...] = dot(rem1[N:392, 0:N], dinv[...])
    snd[0:AUG, :] += dot_nt(e2[N:264, :], rem1[256:384, 0:N])
    rem2[...] = rem1[N:392, N:256] - dot(e2[...], rem1[0:N, N:256])
    dinv[...] = rem2[0:N, :]
    invert(dinv, pbuf)
    h3[...] = dot(rem2[N:264, :], dinv[...])
    snd[0:AUG, :] += dot_nt(h3[...], rem2[N:256, :])
    snd[AUG : AUG + 8, :] = wts[...]

    def y_copy(t):
        return pltpu.make_async_remote_copy(
            src_ref=snd, dst_ref=recv_y.at[t - 1], send_sem=s_y.at[t - 1], recv_sem=r_y.at[t - 1],
            device_id=dev(((y + t) % 4) * 16 + z * 2 + core), device_id_type=MESH,
        )

    for t in (1, 2, 3):
        y_copy(t).start()
    other = 2 * y + 1 - core
    acc_m[...] = snd[0:AUG, :] * snd[pl.ds(AUG + mine, 1), :]
    acc_o[...] = snd[0:AUG, :] * snd[pl.ds(AUG + other, 1), :]
    for t in (1, 3, 2):
        y_copy(t).wait_recv()
        acc_m[...] += recv_y[t - 1, 0:AUG, :] * recv_y[t - 1, pl.ds(AUG + mine, 1), :]
        acc_o[...] += recv_y[t - 1, 0:AUG, :] * recv_y[t - 1, pl.ds(AUG + other, 1), :]
    core_copy = pltpu.make_async_remote_copy(
        src_ref=acc_o, dst_ref=recv_c, send_sem=s_c, recv_sem=r_c,
        device_id=dev(me + 1 - 2 * core), device_id_type=MESH,
    )
    core_copy.start()
    core_copy.wait_recv()
    acc_m[...] += recv_c[...]

    def z_copy(source):
        return pltpu.make_async_remote_copy(
            src_ref=acc_m, dst_ref=recv_z.at[source], send_sem=s_z, recv_sem=r_z.at[source],
            device_id=dev(owner_leaf(mine, own_z)), device_id_type=MESH,
        )

    @pl.when(jnp.logical_not(owner))
    def _():
        z_copy(z).start()

    def slice_copy(src, dst, send_sem, recv_sem, t, by_group):
        if by_group:
            target = (grp + t) % 8
            device = {"leaf": owner_leaf(mine, 4 - target // 4), "grp": target}
            slot = grp
            source = src
        else:
            target = (mine + t) % 8
            device = dev(owner_leaf(target, own_z))
            slot = mine
            source = src
        return pltpu.make_async_remote_copy(
            src_ref=source, dst_ref=dst.at[slot], send_sem=send_sem.at[t], recv_sem=recv_sem.at[slot],
            device_id=device, device_id_type=MESH,
        )

    def slot_wait(dst, send_sem, recv_sem, slot):
        pltpu.make_async_remote_copy(
            src_ref=dst.at[slot], dst_ref=dst.at[slot], send_sem=send_sem.at[0],
            recv_sem=recv_sem.at[slot], device_id=dev(me + 1 - 2 * core), device_id_type=MESH,
        ).wait_recv()

    def message(t):
        return pltpu.make_async_remote_copy(
            src_ref=msg, dst_ref=recv_n.at[mine], send_sem=s_m.at[t], recv_sem=r_m.at[mine],
            device_id=dev((me + t) % 64), device_id_type=MESH,
        )

    @pl.when(owner)
    def _():
        pltpu.make_async_remote_copy(
            src_ref=gath.at[pl.ds(0, 63)], dst_ref=gath.at[pl.ds(0, 63)], send_sem=s_n.at[0],
            recv_sem=r_n, device_id=dev(me + 1 - 2 * core), device_id_type=MESH,
        ).wait_recv()
        rhs = jnp.zeros((4, N), f32)
        for i in range(64):
            tile = gath[i]
            nsys[2 * i : 2 * i + 2, :] = tile[0:2, :]
            nlinks[2 * i : 2 * i + 2, :] = tile[2:4, :]
            rhs = rhs + tile[4:8, :]
        naug[0:N, :] = nlinks[...].T
        acc_m[N : N + 4, :] += -rhs
        acc_m[0:N, :] += nsys[...]
        for t in (1, 7, 2, 6, 3, 5, 4):
            source = (own_z + t) % 8
            z_copy(source).wait_recv()
            acc_m[...] += recv_z[source]
        dinv[...] = acc_m[0:N, :]
        naug[N:AUG, :] = acc_m[N:AUG, :]
        invert(dinv, pbuf)
        hmat[...] = dot(naug[...], dinv[...])
        rparts[...] = dot(hmat[...], nlinks[...])
        for q in range(8):
            send_r[q, 0:16, :] = rparts[16 * q : 16 * q + 16, :]
            send_r[q, 16:24, :] = rparts[N:AUG, :]

        for t in range(1, 8):
            slice_copy(send_r.at[(mine + t) % 8], recv_r, s_r, r_r, t, False).start()
        recv_r[mine] = send_r[mine]
        for t in range(1, 8):
            slot_wait(recv_r, s_r, r_r, (mine + t) % 8)
        total = recv_r[0]
        for q in range(1, 8):
            total = total + recv_r[q]
        part[...] = total
        for t in range(1, 8):
            slice_copy(part, recv_g, s_g, r_g, t, True).start()
        recv_g[grp] = total
        for t in range(1, 8):
            slot_wait(recv_g, s_g, r_g, (grp + t) % 8)
        total = recv_g[0]
        for q in range(1, 8):
            total = total + recv_g[q]
        tot[...] = total
        for t in range(1, 8):
            slice_copy(tot, recv_t, s_t, r_t, t, False).start()
        recv_t[mine] = total
        for t in range(1, 8):
            slot_wait(recv_t, s_t, r_t, (mine + t) % 8)
        for q in range(8):
            dinv[16 * q : 16 * q + 16, :] = rmat[16 * q : 16 * q + 16, :] + recv_t[q, 0:16, :]
        invert(dinv, pbuf)
        root_vec = row_bcast(rrhs[...]) - row_bcast(total[16:17, :])
        root = dot(root_vec, dinv[...])
        node = row_bcast(hmat[N : N + 1, :]) + dot(root, hmat[0:N, :])
        msg[0:1, :] = node[0:1, :]
        msg[1:2, :] = root[0:1, :]

        def send(t, carry):
            message(t).start()
            return carry

        lax.fori_loop(1, 64, send, 0)
        recv_n[mine] = msg[...]

    zt[:, 256:384] = h3[...]
    zt[:, N:256] = e2[N:264, :] - dot(h3[...], e2[0:N, :])
    zt[:, 0:N] = e1[256:392, :] - dot(zt[:, N:384], e1[0:256, :])

    for q in range(8):
        @pl.when(jnp.logical_or(jnp.logical_not(owner), mine != q))
        def _():
            slot_wait(recv_n, s_m, r_m, q)

    parent_dir = jnp.zeros((8, N), f32)
    for q in range(8):
        direction = row_bcast(recv_n[q, 0:1, :])
        parent_dir = parent_dir + direction * row_bcast(wts[q : q + 1, :])
        nd8[q : q + 1, :] = recv_n[q, 0:1, :]
    live = jnp.sum(wts[...], axis=0, keepdims=True)
    moved = dot(parent_dir, zt[0:N, :])
    for b in range(3):
        cols = slice(b * N, (b + 1) * N)
        leaf_out[:, cols] = (zt[N : N + 1, cols] - moved[0:1, cols]) * live
    node_out[...] = pltpu.roll(nd8[...], (N - 2 * me) % N, 1)[:, 0:2]
    root_out[...] = recv_n[0, 1:2, :]

    for q in range(8):
        target = owner_leaf(q, own_z)

        @pl.when(target != me)
        def _():
            node_copy(q, target).wait_send()

    for t in (1, 2, 3):
        y_copy(t).wait_send()
    core_copy.wait_send()

    @pl.when(jnp.logical_not(owner))
    def _():
        z_copy(z).wait_send()

    @pl.when(owner)
    def _():
        for t in range(1, 8):
            slice_copy(send_r.at[(mine + t) % 8], recv_r, s_r, r_r, t, False).wait_send()
            slice_copy(part, recv_g, s_g, r_g, t, True).wait_send()
            slice_copy(tot, recv_t, s_t, r_t, t, False).wait_send()

        def drain(t, carry):
            message(t).wait_send()
            return carry

        lax.fori_loop(1, 64, drain, 0)


def body(
    slot_parent, leaf_matrix, coupling, leaf_residual_rows, node_matrix, node_link, node_rhs,
    root_matrix, root_rhs,
):
    vmem = pl.BlockSpec(memory_space=pltpu.VMEM)
    buf = lambda *shape: pltpu.VMEM(shape, f32)
    dma = pltpu.SemaphoreType.DMA
    leaf_dir, node_dir, root_dir = pl.pallas_call(
        kernel,
        out_shape=(
            jax.ShapeDtypeStruct((1, 384), f32),
            jax.ShapeDtypeStruct((8, 2), f32),
            jax.ShapeDtypeStruct((1, N), f32),
        ),
        in_specs=[pl.BlockSpec(memory_space=pltpu.SMEM)] + [vmem] * 8,
        out_specs=(vmem, vmem, vmem),
        scratch_shapes=[
            buf(AUG, 384), buf(N, N), buf(64, N), buf(392, N), buf(392, 256), buf(264, N),
            buf(264, N), buf(AUG, N), buf(8, N),
            buf(8, 8, N), buf(64, 8, N), buf(144, N), buf(3, 144, N), buf(AUG, N), buf(AUG, N),
            buf(AUG, N), buf(8, AUG, N),
            buf(N, N), buf(N, N), buf(AUG, N), buf(AUG, N), buf(AUG, N), buf(8, 24, N),
            buf(8, 24, N), buf(24, N), buf(8, 24, N), buf(24, N), buf(8, 24, N),
            buf(2, N), buf(8, 2, N), buf(AUG, 384), buf(8, N),
            dma((8,)), dma, dma((3,)), dma((3,)), dma, dma, dma, dma((8,)),
            dma((8,)), dma((8,)), dma((8,)), dma((8,)), dma((8,)), dma((8,)), dma((64,)), dma((8,)),
        ],
        compiler_params=pltpu.CompilerParams(collective_id=0, has_side_effects=True),
        name="newton_step",
    )(
        slot_parent, leaf_matrix, coupling, leaf_residual_rows, node_matrix, node_link, node_rhs,
        root_matrix, root_rhs[None, :],
    )
    return leaf_dir, node_dir, root_dir[0]


def solution(mesh):
    return jax.shard_map(
        body,
        mesh=mesh,
        in_specs=(
            P(("leaf", "grp")),
            P(("leaf", "grp"), None, None),
            P(("leaf", "grp"), None, None),
            P(("leaf", "grp"), None),
            P("grp", "leaf", None),
            P("grp", "leaf", None),
            P("grp", "leaf"),
            P(),
            P(),
        ),
        out_specs=(P(("leaf", "grp"), None), P("grp", "leaf"), P()),
        check_vma=False,
    )
```

time: 1320 us -> 85.3 us (0.06); the launches traced: 1310 us -> 85.1 us
  blocking collectives: 583 us -> 0 us
  waiting for transfers between devices: 395 us -> 0 us
  other arithmetic: 284 us -> 0 us
  Pallas kernels: 0 us -> 80 us
  between operations: 17.6 us -> 1.3 us
    psum x2 -> x0, blocking collectives: 458 us -> none  [the longest x1 423 us: body(): schur, node_vec = lax.psum((partial_schur, partial_vec), 'leaf')]
    psum x2 -> x0, waiting for transfers between devices: 394 us -> none  [the longest x1 286 us: body(): schur, node_vec = lax.psum((partial_schur, partial_vec), 'leaf')]
    another operation x27 -> x0, other arithmetic: 281 us -> none  [the longest x7 119 us: upper_solve(): lax.linalg.triangular_solve(factor, values, left_side=True, lower=True, t...]
    all_gather x1 -> x0, blocking collectives: 125 us -> none  [body(): links = lax.all_gather(node_link, 'leaf', axis=1, tiled=True)]
    pallas_call x0 -> x1, Pallas kernels: none -> 80 us  [body(): pl.pallas_call(kernel, out_shape=(jax.ShapeDtypeStruct((1, 384), f32), ja...]
  transfers between devices with their start and end apart: 2 -> 0, of which waited for: 2 -> 0; matrix products, arithmetic and copies ran while one was open for 0% -> 0% of each run, Pallas kernels for 0% -> 0%
where the time goes in v1:
time: 85.3 us; the launch traced here: 85.1 us
  Pallas kernels  80 us (94%)
  local copies, waits for them, and re-layouts  3.81 us (4%)
  between operations  1.3 us (2%)
    pallas_call x1, Pallas kernels, body(): pl.pallas_call(kernel, out_shape=(jax.ShapeDtypeStruct((1, 384), f32), ja...  80 us
    unnamed x12, local copies, waits for them, and re-layouts  3.81 us

profile of v1, /device:TPU:1, one launch (start us, length us, event | category | flops | bytes accessed | tf_op | source)
XLA Modules:
  0.0 85.1 jit_solution(18439302278729213356)
XLA Ops:
  1.3 0.0 copy-start.2
  1.3 0.7 copy-done.2
  2.0 0.7 copy.12.nrhs
  2.6 80.0 %newton_step.1 = (f32[1,384]{1,0:T(1,128)}, f32[8,2]{1,0:T(8,128)}, f32[1,128]{1,0:T(1,128)}) custom-call(s32[1]{0:T(128)S(6)} %copy.16.parent, f32[1,384,384]{2,1,0:T(8,128)} %amat.1, f32[1,384,128]{2,1,0:T(8,128)} %coup.1, f32[1,384]{1,0:T(1,128)} %resid.1, f32[8,2,128]{2,1,0:T(2,128)} %nmat.1, f32[8,2,128]{2,1,0:T(2,128)} %nlink.1, f32[8,2]{1,0:T(8,128)} %copy.12.nrhs, ...), custom_call_target="tpu_custom_call" | custom-call | tf_op jit(solution)/shard_map/newton_step/pallas_call | solution.py:385
  82.6 0.0 copy-start
  82.6 0.7 copy-done
  83.3 0.0 copy-start.1
  83.3 0.6 copy.13
  83.9 0.0 copy-done.1
  84.0 0.0 copy-start.3
  84.0 0.6 copy.17
  84.5 0.0 copy-done.3
  84.6 0.5 copy.18
Async XLA Ops:
  1.3 0.7 copy-start.2
  82.6 0.7 copy-start
  83.3 0.7 copy-start.1
  84.0 0.6 copy-start.3

commit v2 on v1

v2 whole, which is shorter than its diff:
```python
import jax
import jax.numpy as jnp
from jax import lax
from jax.experimental import pallas as pl
from jax.experimental.pallas import tpu as pltpu
from jax.sharding import PartitionSpec as P

f32 = jnp.float32
MESH = pl.DeviceIdType.MESH
HI = lax.Precision.HIGHEST
N = 128
AUG = 136


def dot(a, b):
    return jnp.dot(a, b, precision=HI, preferred_element_type=f32)


def dot_nt(a, b):
    return lax.dot_general(
        a, b, (((1,), (1,)), ((), ())), precision=HI, preferred_element_type=f32
    )


def lane_bcast(x, index):
    dims = lax.GatherDimensionNumbers(
        offset_dims=(), collapsed_slice_dims=(1,), start_index_map=(1,),
        operand_batching_dims=(0,), start_indices_batching_dims=(0,),
    )
    return lax.gather(
        x, index[:, :, None], dims, (1, 1), mode=lax.GatherScatterMode.PROMISE_IN_BOUNDS
    )


def row_bcast(row):
    return jnp.broadcast_to(row, (8, N))


def invert(d_ref, p_ref, q_ref):
    lane = lax.broadcasted_iota(jnp.int32, (8, N), 1)
    sub = lax.broadcasted_iota(jnp.int32, (8, N), 0)
    half = N // 2
    for h in (0, 1):
        top = h * half
        first = d_ref[top : top + 8, :]
        for j in range(8):
            p_ref[8 * j : 8 * j + 8, :] = lane_bcast(first, jnp.full((8, N), top + j, jnp.int32))

        def block(k, carry):
            base = pl.multiple_of(top + k * 8, 8)
            base_next = pl.multiple_of(top + jnp.minimum(k + 1, 7) * 8, 8)
            here = [jnp.full((8, N), base + j, jnp.int32) for j in range(8)]
            after = [jnp.full((8, N), base_next + j, jnp.int32) for j in range(8)]
            s = {}
            for j in range(8):
                for i in range(j + 1):
                    s[i, j] = row_bcast(p_ref[8 * j + i : 8 * j + i + 1, :])
            r = [row_bcast(d_ref[pl.ds(base + j, 1), :]) for j in range(8)]
            d = [d_ref[top + g * 8 : top + (g + 1) * 8, :] for g in range(8)]
            dn = d_ref[pl.ds(base_next, 8), :]
            cn, pn, c = [], [], []
            for j in range(8):
                cn.append(lane_bcast(dn, here[j]))
            for j in range(8):
                pn.append(lane_bcast(dn, after[j]))
            for j in range(8):
                c.append([lane_bcast(d[g], here[j]) for g in range(8)])
            inside = (lane >= base) & (lane < base + 8)
            r = [jnp.where(inside, jnp.where(lane == base + j, 1.0, 0.0), r[j]) for j in range(8)]
            low, inv = {}, []
            for j in range(8):
                inv.append(1.0 / s[j, j])
                for i in range(j + 1, 8):
                    low[i, j] = s[j, i] * inv[j]
                for i in range(j + 1, 8):
                    for m in range(i, 8):
                        s[i, m] = s[i, m] - low[i, j] * s[j, m]
                q_ref[8 * j : 8 * j + 8, :] = cn[j]
                scaled = cn[j] * inv[j]
                for i in range(8):
                    pn[i] = pn[i] - scaled * row_bcast(q_ref[8 * j + i : 8 * j + i + 1, :])
                for i in range(j + 1, 8):
                    cn[i] = cn[i] - low[i, j] * cn[j]
                for i in range(j + 1, 8):
                    r[i] = r[i] - low[i, j] * r[j]
            for j in range(8):
                p_ref[8 * j : 8 * j + 8, :] = pn[j]
            x = [r[j] * inv[j] for j in range(8)]
            for j in range(7, -1, -1):
                for i in range(j):
                    x[i] = x[i] - low[j, i] * x[j]
            for g in range(8):
                kept = jnp.where(inside, 0.0, d[g])
                t = [c[j][g] * x[j] for j in range(8)]
                d_ref[top + g * 8 : top + (g + 1) * 8, :] = kept - (
                    ((t[0] + t[1]) + (t[2] + t[3])) + ((t[4] + t[5]) + (t[6] + t[7]))
                )
            new = x[0]
            for j in range(1, 8):
                new = jnp.where(sub == j, x[j], new)
            d_ref[pl.ds(base, 8), :] = new
            return carry

        lax.fori_loop(0, 8, block, 0)
        wide = lax.broadcasted_iota(jnp.int32, (half, N), 1)
        if h == 0:
            rest = d_ref[half:N, :]
            d_ref[half:N, :] = jnp.where(wide < half, 0.0, rest) - dot(rest[:, 0:half], d_ref[0:half, :])
        else:
            rest = d_ref[0:half, :]
            d_ref[0:half, :] = jnp.where(wide < half, rest, 0.0) - dot(
                jnp.where(wide < half, 0.0, rest), d_ref[...]
            )


def kernel(
    parent, amat, coup, resid, nmat, nlink, nrhs, rmat, rrhs,
    packed,
    av, cv, bt, dinv, pbuf, qbuf, e1, rem1, e2, rem2, h3, wts,
    ntile, gath, snd, recv_y, acc_o, recv_c, acc_m, recv_z,
    nsys, nlinks, naug, hmat, rparts, send_r, recv_r, part, recv_g, tot, recv_t,
    msg, recv_n, zt, nd8,
    s_l, s_n, r_n, s_y, r_y, s_c, r_c, s_z, r_z, s_r, r_r, s_g, r_g, s_t, r_t, s_m, r_m,
):
    me = lax.axis_index("leaf")
    grp = lax.axis_index("grp")
    y, z, core = me // 16, (me // 2) % 8, me % 2
    own_z = 4 - grp // 4
    owner = z == own_z
    mine = 2 * y + core

    def dev(leaf):
        return {"leaf": leaf, "grp": grp}

    def owner_leaf(m, oz):
        return (m // 2) * 16 + oz * 2 + m % 2

    local = [
        pltpu.make_async_copy(amat.at[0, pl.ds(0, N), pl.ds(0, N)], dinv, s_l.at[0]),
        pltpu.make_async_copy(amat.at[0], av, s_l.at[1]),
        pltpu.make_async_copy(coup.at[0], cv, s_l.at[2]),
    ]
    for copy in local:
        copy.start()

    barrier = pltpu.get_barrier_semaphore()

    def greet(t, carry):
        pl.semaphore_signal(barrier, inc=1, device_id=dev((me + t) % 64), device_id_type=MESH)
        return carry

    lax.fori_loop(1, 64, greet, 0)

    @pl.when(owner)
    def _():
        def greet_far(t, carry):
            g = (grp + t) % 8
            pl.semaphore_signal(
                barrier, inc=1,
                device_id={"leaf": owner_leaf(mine, 4 - g // 4), "grp": g}, device_id_type=MESH,
            )
            return carry

        lax.fori_loop(1, 8, greet_far, 0)

    local[0].wait()
    invert(dinv, pbuf, qbuf)

    sub = lax.broadcasted_iota(jnp.int32, (8, N), 0)
    lane = lax.broadcasted_iota(jnp.int32, (8, N), 1)
    sub4 = lax.broadcasted_iota(jnp.int32, (4, N), 0)
    lane4 = lax.broadcasted_iota(jnp.int32, (4, N), 1)
    wts[...] = jnp.where(sub == parent[0], 1.0, 0.0)
    nd8[...] = jnp.zeros((8, N), f32)
    nd8[0:2, 0:8] = nrhs[...]
    pair = nd8[...]
    for q in range(8):
        value = lane_bcast(pair, jnp.full((8, N), q, jnp.int32))
        ntile[q, 0:2, :] = nmat[q]
        ntile[q, 2:4, :] = nlink[q]
        ntile[q, 4:8, :] = jnp.where(
            sub4 == 0,
            jnp.where(lane4 == 2 * me, value[0:1, :], 0.0)
            + jnp.where(lane4 == 2 * me + 1, value[1:2, :], 0.0),
            0.0,
        )

    @pl.when(owner)
    def _():
        pl.semaphore_wait(barrier, 70)

    @pl.when(jnp.logical_not(owner))
    def _():
        pl.semaphore_wait(barrier, 63)

    def node_copy(q, target):
        return pltpu.make_async_remote_copy(
            src_ref=ntile.at[q], dst_ref=gath.at[me], send_sem=s_n.at[q], recv_sem=r_n,
            device_id=dev(target), device_id_type=MESH,
        )

    for q in range(8):
        target = owner_leaf(q, own_z)

        @pl.when(target != me)
        def _():
            node_copy(q, target).start()

        @pl.when(target == me)
        def _():
            gath[me] = ntile[q]

    local[1].wait()
    local[2].wait()
    for b in range(3):
        bt[0:N, b * N : (b + 1) * N] = cv[b * N : (b + 1) * N, :].T
        bt[N:AUG, b * N : (b + 1) * N] = jnp.where(
            sub == 0, row_bcast(resid[:, b * N : (b + 1) * N]), 0.0
        )
    d1 = dinv[...]
    e1[0:256, :] = dot(av[N:384, 0:N], d1)
    e1[256:392, :] = dot(bt[:, 0:N], d1)
    snd[0:AUG, :] = dot_nt(e1[256:392, :], bt[0:N, 0:N])
    rem1[0:256, :] = av[N:384, N:384] - dot(e1[0:256, :], av[0:N, N:384])
    rem1[256:392, :] = bt[:, N:384] - dot(e1[256:392, :], av[0:N, N:384])
    dinv[...] = rem1[0:N, 0:N]
    invert(dinv, pbuf, qbuf)
    e2[...] = dot(rem1[N:392, 0:N], dinv[...])
    snd[0:AUG, :] += dot_nt(e2[N:264, :], rem1[256:384, 0:N])
    rem2[...] = rem1[N:392, N:256] - dot(e2[...], rem1[0:N, N:256])
    dinv[...] = rem2[0:N, :]
    invert(dinv, pbuf, qbuf)
    h3[...] = dot(rem2[N:264, :], dinv[...])
    snd[0:AUG, :] += dot_nt(h3[...], rem2[N:256, :])
    snd[AUG : AUG + 8, :] = wts[...]

    def y_copy(step, slot, part, src, sem):
        rows = pl.ds(72 * part, 72)
        return pltpu.make_async_remote_copy(
            src_ref=src.at[rows], dst_ref=recv_y.at[slot, rows], send_sem=s_y.at[sem],
            recv_sem=r_y.at[2 * slot + part],
            device_id=dev(((y + step + 4) % 4) * 16 + z * 2 + core), device_id_type=MESH,
        )

    up_a, up_b = y_copy(1, 0, 0, snd, 0), y_copy(1, 0, 1, snd, 1)
    down_b, down_a = y_copy(-1, 2, 1, snd, 2), y_copy(-1, 2, 0, snd, 3)
    pass_a = y_copy(1, 1, 0, recv_y.at[0], 4)
    pass_b = y_copy(-1, 1, 1, recv_y.at[2], 5)
    for copy in (up_a, down_b, up_b, down_a):
        copy.start()
    other = 2 * y + 1 - core
    acc_m[...] = snd[0:AUG, :] * snd[pl.ds(AUG + mine, 1), :]
    acc_o[...] = snd[0:AUG, :] * snd[pl.ds(AUG + other, 1), :]
    up_a.wait_recv()
    pass_a.start()
    down_b.wait_recv()
    pass_b.start()
    for slot, copies in ((0, (up_b,)), (2, (down_a,)), (1, (pass_a, pass_b))):
        for copy in copies:
            copy.wait_recv()
        acc_m[...] += recv_y[slot, 0:AUG, :] * recv_y[slot, pl.ds(AUG + mine, 1), :]
        acc_o[...] += recv_y[slot, 0:AUG, :] * recv_y[slot, pl.ds(AUG + other, 1), :]
    core_copy = pltpu.make_async_remote_copy(
        src_ref=acc_o, dst_ref=recv_c, send_sem=s_c, recv_sem=r_c,
        device_id=dev(me + 1 - 2 * core), device_id_type=MESH,
    )
    core_copy.start()
    core_copy.wait_recv()
    acc_m[...] += recv_c[...]

    def z_copy(source):
        return pltpu.make_async_remote_copy(
            src_ref=acc_m, dst_ref=recv_z.at[source], send_sem=s_z, recv_sem=r_z.at[source],
            device_id=dev(owner_leaf(mine, own_z)), device_id_type=MESH,
        )

    @pl.when(jnp.logical_not(owner))
    def _():
        z_copy(z).start()

    def slice_copy(src, dst, send_sem, recv_sem, t, by_group):
        if by_group:
            target = (grp + t) % 8
            device = {"leaf": owner_leaf(mine, 4 - target // 4), "grp": target}
            slot = grp
            source = src
        else:
            target = (mine + t) % 8
            device = dev(owner_leaf(target, own_z))
            slot = mine
            source = src
        return pltpu.make_async_remote_copy(
            src_ref=source, dst_ref=dst.at[slot], send_sem=send_sem.at[t], recv_sem=recv_sem.at[slot],
            device_id=device, device_id_type=MESH,
        )

    def slot_wait(dst, send_sem, recv_sem, slot):
        pltpu.make_async_remote_copy(
            src_ref=dst.at[slot], dst_ref=dst.at[slot], send_sem=send_sem.at[0],
            recv_sem=recv_sem.at[slot], device_id=dev(me + 1 - 2 * core), device_id_type=MESH,
        ).wait_recv()

    def message(far, t):
        plane = far + (7 - 2 * far) * (grp // 4)
        target = (mine + t) % 8
        return pltpu.make_async_remote_copy(
            src_ref=msg, dst_ref=recv_n.at[mine], send_sem=s_m.at[far, t], recv_sem=r_m.at[mine],
            device_id=dev((target // 2) * 16 + plane * 2 + target % 2), device_id_type=MESH,
        )

    @pl.when(owner)
    def _():
        pltpu.make_async_remote_copy(
            src_ref=gath.at[pl.ds(0, 63)], dst_ref=gath.at[pl.ds(0, 63)], send_sem=s_n.at[0],
            recv_sem=r_n, device_id=dev(me + 1 - 2 * core), device_id_type=MESH,
        ).wait_recv()
        rhs = jnp.zeros((4, N), f32)
        for i in range(64):
            tile = gath[i]
            nsys[2 * i : 2 * i + 2, :] = tile[0:2, :]
            nlinks[2 * i : 2 * i + 2, :] = tile[2:4, :]
            rhs = rhs + tile[4:8, :]
        naug[0:N, :] = nlinks[...].T
        acc_m[N : N + 4, :] += -rhs
        acc_m[0:N, :] += nsys[...]
        for t in (1, 7, 2, 6, 3, 5, 4):
            source = (own_z + t) % 8
            z_copy(source).wait_recv()
            acc_m[...] += recv_z[source]
        dinv[...] = acc_m[0:N, :]
        naug[N:AUG, :] = acc_m[N:AUG, :]
        invert(dinv, pbuf, qbuf)
        hmat[...] = dot(naug[...], dinv[...])
        rparts[...] = dot(hmat[...], nlinks[...])
        for q in range(8):
            send_r[q, 0:16, :] = rparts[16 * q : 16 * q + 16, :]
            send_r[q, 16:24, :] = rparts[N:AUG, :]

        for t in range(1, 8):
            slice_copy(send_r.at[(mine + t) % 8], recv_r, s_r, r_r, t, False).start()
        recv_r[mine] = send_r[mine]
        for t in range(1, 8):
            slot_wait(recv_r, s_r, r_r, (mine + t) % 8)
        total = recv_r[0]
        for q in range(1, 8):
            total = total + recv_r[q]
        part[...] = total
        for t in range(1, 8):
            slice_copy(part, recv_g, s_g, r_g, t, True).start()
        recv_g[grp] = total
        for t in range(1, 8):
            slot_wait(recv_g, s_g, r_g, (grp + t) % 8)
        total = recv_g[0]
        for q in range(1, 8):
            total = total + recv_g[q]
        tot[...] = total
        for t in range(1, 8):
            slice_copy(tot, recv_t, s_t, r_t, t, False).start()
        recv_t[mine] = total
        for t in range(1, 8):
            slot_wait(recv_t, s_t, r_t, (mine + t) % 8)
        for q in range(8):
            dinv[16 * q : 16 * q + 16, :] = rmat[16 * q : 16 * q + 16, :] + recv_t[q, 0:16, :]
        invert(dinv, pbuf, qbuf)
        root_vec = row_bcast(rrhs[...]) - row_bcast(total[16:17, :])
        root = dot(root_vec, dinv[...])
        node = row_bcast(hmat[N : N + 1, :]) + dot(root, hmat[0:N, :])
        msg[0:1, :] = node[0:1, :]
        msg[1:2, :] = root[0:1, :]

        for far in (0, 1, 7, 2, 6, 3, 5, 4):
            def send(t, carry):
                message(far, t).start()
                return carry

            lax.fori_loop(1 if far == 4 else 0, 8, send, 0)
        recv_n[mine] = msg[...]

    zt[:, 256:384] = h3[...]
    zt[:, N:256] = e2[N:264, :] - dot(h3[...], e2[0:N, :])
    zt[:, 0:N] = e1[256:392, :] - dot(zt[:, N:384], e1[0:256, :])

    @pl.when(owner)
    def _():
        for far in range(8):
            def drain(t, carry):
                message(far, t).wait_send()
                return carry

            lax.fori_loop(1 if far == 4 else 0, 8, drain, 0)

    for q in range(8):
        @pl.when(jnp.logical_or(jnp.logical_not(owner), mine != q))
        def _():
            slot_wait(recv_n, s_m, r_m, q)

    parent_dir = jnp.zeros((8, N), f32)
    for q in range(8):
        direction = row_bcast(recv_n[q, 0:1, :])
        parent_dir = parent_dir + direction * row_bcast(wts[q : q + 1, :])
        nd8[q : q + 1, :] = recv_n[q, 0:1, :]
    live = jnp.sum(wts[...], axis=0, keepdims=True)
    moved = dot(parent_dir, zt[0:N, :])
    for b in range(3):
        cols = slice(b * N, (b + 1) * N)
        packed[b : b + 1, :] = (zt[N : N + 1, cols] - moved[0:1, cols]) * live
    packed[3:4, :] = recv_n[0, 1:2, :]
    for a in range(2):
        values = lane_bcast(nd8[...], jnp.full((8, N), 2 * me + a, jnp.int32))
        packed[4 + a : 5 + a, :] = jnp.sum(jnp.where(sub == lane, values, 0.0), axis=0, keepdims=True)
    packed[6:8, :] = jnp.zeros((2, N), f32)

    for q in range(8):
        target = owner_leaf(q, own_z)

        @pl.when(target != me)
        def _():
            node_copy(q, target).wait_send()

    for copy in (up_a, up_b, down_a, down_b, pass_a, pass_b):
        copy.wait_send()
    core_copy.wait_send()

    @pl.when(jnp.logical_not(owner))
    def _():
        z_copy(z).wait_send()

    @pl.when(owner)
    def _():
        for t in range(1, 8):
            slice_copy(send_r.at[(mine + t) % 8], recv_r, s_r, r_r, t, False).wait_send()
            slice_copy(part, recv_g, s_g, r_g, t, True).wait_send()
            slice_copy(tot, recv_t, s_t, r_t, t, False).wait_send()


def unpack(packed, leaf_out, node_out, root_out):
    for b in range(3):
        leaf_out[:, b * N : (b + 1) * N] = packed[b : b + 1, :]
    node_out[...] = packed[4:6, 0:8]
    root_out[...] = packed[3:4, :]


def body(
    slot_parent, leaf_matrix, coupling, leaf_residual_rows, node_matrix, node_link, node_rhs,
    root_matrix, root_rhs,
):
    vmem = pl.BlockSpec(memory_space=pltpu.VMEM)
    buf = lambda *shape: pltpu.VMEM(shape, f32)
    dma = pltpu.SemaphoreType.DMA
    packed = pl.pallas_call(
        kernel,
        out_shape=jax.ShapeDtypeStruct((8, N), f32),
        in_specs=[
            pl.BlockSpec(memory_space=pltpu.SMEM), pl.BlockSpec(memory_space=pl.ANY),
            pl.BlockSpec(memory_space=pl.ANY),
        ] + [vmem] * 6,
        out_specs=vmem,
        scratch_shapes=[
            buf(384, 384), buf(384, N),
            buf(AUG, 384), buf(N, N), buf(64, N), buf(64, N), buf(392, N), buf(392, 256), buf(264, N),
            buf(264, N), buf(AUG, N), buf(8, N),
            buf(8, 8, N), buf(64, 8, N), buf(144, N), buf(3, 144, N), buf(AUG, N), buf(AUG, N),
            buf(AUG, N), buf(8, AUG, N),
            buf(N, N), buf(N, N), buf(AUG, N), buf(AUG, N), buf(AUG, N), buf(8, 24, N),
            buf(8, 24, N), buf(24, N), buf(8, 24, N), buf(24, N), buf(8, 24, N),
            buf(2, N), buf(8, 2, N), buf(AUG, 384), buf(8, N),
            dma((3,)), dma((8,)), dma, dma((6,)), dma((6,)), dma, dma, dma, dma((8,)),
            dma((8,)), dma((8,)), dma((8,)), dma((8,)), dma((8,)), dma((8,)), dma((8, 8)), dma((8,)),
        ],
        compiler_params=pltpu.CompilerParams(collective_id=0, has_side_effects=True),
        name="newton_step",
    )(
        slot_parent, leaf_matrix, coupling, leaf_residual_rows, node_matrix, node_link, node_rhs.T,
        root_matrix, root_rhs[None, :],
    )
    leaf_dir, node_dir, root_dir = pl.pallas_call(
        unpack,
        out_shape=(
            jax.ShapeDtypeStruct((1, 384), f32),
            jax.ShapeDtypeStruct((2, 8), f32),
            jax.ShapeDtypeStruct((1, N), f32),
        ),
        in_specs=[vmem],
        out_specs=(vmem, vmem, vmem),
        name="unpack",
    )(packed)
    return leaf_dir, node_dir.T, root_dir[0]


def solution(mesh):
    return jax.shard_map(
        body,
        mesh=mesh,
        in_specs=(
            P(("leaf", "grp")),
            P(("leaf", "grp"), None, None),
            P(("leaf", "grp"), None, None),
            P(("leaf", "grp"), None),
            P("grp", "leaf", None),
            P("grp", "leaf", None),
            P("grp", "leaf"),
            P(),
            P(),
        ),
        out_specs=(P(("leaf", "grp"), None), P("grp", "leaf"), P()),
        check_vma=False,
    )
```

time: 85.3 us -> 78.6 us (0.921)
  local copies, waits for them, and re-layouts: 3.81 us -> 0 us
  Pallas kernels: 80 us -> 77.1 us
    unnamed x12 -> x0, local copies, waits for them, and re-layouts: 3.81 us -> none
    pallas_call x1 -> x2, Pallas kernels: 80 us -> 77.1 us  [the longest x1 75.9 us: body(): pl.pallas_call(kernel, out_shape=jax.ShapeDtypeStruct((8, N), f32), in_sp...]
where the time goes in v2:
time: 78.6 us; the launch traced here: 78.4 us
  Pallas kernels  77.1 us (98%)
  between operations  1.29 us (2%)
    pallas_call x1, Pallas kernels, body(): pl.pallas_call(kernel, out_shape=jax.ShapeDtypeStruct((8, N), f32), in_sp...  75.9 us

profile of v2, /device:TPU:1, one launch (start us, length us, event | category | flops | bytes accessed | tf_op | source)
XLA Modules:
  0.0 78.4 jit_solution(5910373339301953880)
XLA Ops:
  1.3 75.9 %newton_step.1.packed = f32[8,128]{1,0:T(8,128)} custom-call(s32[1]{0:T(128)S(6)} %copy.12.parent, f32[1,384,384]{2,1,0:T(8,128)} %amat.1, f32[1,384,128]{2,1,0:T(8,128)} %coup.1, f32[1,384]{1,0:T(1,128)} %resid.1, f32[8,2,128]{2,1,0:T(2,128)} %nmat.1, f32[8,2,128]{2,1,0:T(2,128)} %nlink.1, f32[2,8]{1,0:T(2,128)} %bitcast.4, f32[128,128]{1,0:T(8,128)} %rmat.1, ...), custom_call_target="tpu_custom_call" | custom-call | tf_op jit(solution)/shard_map/newton_step/pallas_call | solution.py:450
  77.2 1.2 %unpack.1 = (f32[1,384]{1,0:T(1,128)}, f32[2,8]{1,0:T(2,128)}, f32[1,128]{1,0:T(1,128)}) custom-call(f32[8,128]{1,0:T(8,128)} %newton_step.1.packed), custom_call_target="tpu_custom_call" | custom-call | tf_op jit(solution)/shard_map/unpack/pallas_call | solution.py:476

commit v3 on v2

--- a/solution.py
+++ b/solution.py
@@ -10,6 +10,8 @@
 HI = lax.Precision.HIGHEST
 N = 128
 AUG = 136
+PANEL = 64
+GROUPS = PANEL // 8
 
 
 def dot(a, b):
@@ -39,16 +41,15 @@
 def invert(d_ref, p_ref, q_ref):
     lane = lax.broadcasted_iota(jnp.int32, (8, N), 1)
     sub = lax.broadcasted_iota(jnp.int32, (8, N), 0)
-    half = N // 2
-    for h in (0, 1):
-        top = h * half
+    for h in range(N // PANEL):
+        top = h * PANEL
         first = d_ref[top : top + 8, :]
         for j in range(8):
             p_ref[8 * j : 8 * j + 8, :] = lane_bcast(first, jnp.full((8, N), top + j, jnp.int32))
 
-        def block(k, carry):
-            base = pl.multiple_of(top + k * 8, 8)
-            base_next = pl.multiple_of(top + jnp.minimum(k + 1, 7) * 8, 8)
+        for k in range(GROUPS):
+            base = top + k * 8
+            base_next = top + min(k + 1, GROUPS - 1) * 8
             here = [jnp.full((8, N), base + j, jnp.int32) for j in range(8)]
             after = [jnp.full((8, N), base_next + j, jnp.int32) for j in range(8)]
             s = {}
@@ -56,7 +57,7 @@
                 for i in range(j + 1):
                     s[i, j] = row_bcast(p_ref[8 * j + i : 8 * j + i + 1, :])
             r = [row_bcast(d_ref[pl.ds(base + j, 1), :]) for j in range(8)]
-            d = [d_ref[top + g * 8 : top + (g + 1) * 8, :] for g in range(8)]
+            d = [d_ref[top + g * 8 : top + (g + 1) * 8, :] for g in range(GROUPS)]
             dn = d_ref[pl.ds(base_next, 8), :]
             cn, pn, c = [], [], []
             for j in range(8):
@@ -64,7 +65,7 @@
             for j in range(8):
                 pn.append(lane_bcast(dn, after[j]))
             for j in range(8):
-                c.append([lane_bcast(d[g], here[j]) for g in range(8)])
+                c.append([lane_bcast(d[g], here[j]) for g in range(GROUPS)])
             inside = (lane >= base) & (lane < base + 8)
             r = [jnp.where(inside, jnp.where(lane == base + j, 1.0, 0.0), r[j]) for j in range(8)]
             low, inv = {}, []
@@ -89,7 +90,7 @@
             for j in range(7, -1, -1):
                 for i in range(j):
                     x[i] = x[i] - low[j, i] * x[j]
-            for g in range(8):
+            for g in range(GROUPS):
                 kept = jnp.where(inside, 0.0, d[g])
                 t = [c[j][g] * x[j] for j in range(8)]
                 d_ref[top + g * 8 : top + (g + 1) * 8, :] = kept - (
@@ -99,26 +100,28 @@
             for j in range(1, 8):
                 new = jnp.where(sub == j, x[j], new)
             d_ref[pl.ds(base, 8), :] = new
-            return carry
-
-        lax.fori_loop(0, 8, block, 0)
-        wide = lax.broadcasted_iota(jnp.int32, (half, N), 1)
-        if h == 0:
-            rest = d_ref[half:N, :]
-            d_ref[half:N, :] = jnp.where(wide < half, 0.0, rest) - dot(rest[:, 0:half], d_ref[0:half, :])
+        pan = d_ref[top : top + PANEL, :]
+        wide = lax.broadcasted_iota(jnp.int32, (N - PANEL, N), 1)
+        in_pan = (wide >= top) & (wide < top + PANEL)
+        if top == 0:
+            rest = d_ref[PANEL:N, :]
+        elif top + PANEL == N:
+            rest = d_ref[0:top, :]
         else:
-            rest = d_ref[0:half, :]
-            d_ref[0:half, :] = jnp.where(wide < half, rest, 0.0) - dot(
-                jnp.where(wide < half, 0.0, rest), d_ref[...]
-            )
+            rest = jnp.concatenate([d_ref[0:top, :], d_ref[top + PANEL : N, :]], axis=0)
+        out = jnp.where(in_pan, 0.0, rest) - dot(rest[:, top : top + PANEL], pan)
+        if top > 0:
+            d_ref[0:top, :] = out[0:top, :]
+        if top + PANEL < N:
+            d_ref[top + PANEL : N, :] = out[top : N - PANEL, :]
 
 
 def kernel(
     parent, amat, coup, resid, nmat, nlink, nrhs, rmat, rrhs,
     packed,
-    av, cv, bt, dinv, pbuf, qbuf, e1, rem1, e2, rem2, h3, wts,
+    av, cv, bt, dinv, dinv2, dinv3, pbuf, qbuf, pbuf2, qbuf2, e1, rem1, e2, rem2, h3, wts,
     ntile, gath, snd, recv_y, acc_o, recv_c, acc_m, recv_z,
-    nsys, nlinks, naug, hmat, rparts, send_r, recv_r, part, recv_g, tot, recv_t,
+    nsys, nvec, nlinks, naug, hmat, rparts, send_r, recv_r, part, recv_g, tot, recv_t,
     msg, recv_n, zt, nd8,
     s_l, s_n, r_n, s_y, r_y, s_c, r_c, s_z, r_z, s_r, r_r, s_g, r_g, s_t, r_t, s_m, r_m,
 ):
@@ -217,21 +220,22 @@
         bt[N:AUG, b * N : (b + 1) * N] = jnp.where(
             sub == 0, row_bcast(resid[:, b * N : (b + 1) * N]), 0.0
         )
-    d1 = dinv[...]
-    e1[0:256, :] = dot(av[N:384, 0:N], d1)
-    e1[256:392, :] = dot(bt[:, 0:N], d1)
+    e1[0:N, :] = dot(av[N:256, 0:N], dinv[...])
+    dinv2[...] = av[N:256, N:256] - dot(e1[0:N, :], av[0:N, N:256])
+    e1[N:392, :] = dot(jnp.concatenate([av[256:384, 0:N], bt[:, 0:N]], axis=0), dinv[...])
+    rem1[0:N, N:256] = av[N:256, 256:384] - dot(e1[0:N, :], av[0:N, 256:384])
+    rem1[N:256, :] = av[256:384, N:384] - dot(e1[N:256, :], av[0:N, N:384])
+    rem1[256:392, :] = bt[:, N:384] - dot(e1[256:392, :], av[0:N, N:384])
     snd[0:AUG, :] = dot_nt(e1[256:392, :], bt[0:N, 0:N])
-    rem1[0:256, :] = av[N:384, N:384] - dot(e1[0:256, :], av[0:N, N:384])
-    rem1[256:392, :] = bt[:, N:384] - dot(e1[256:392, :], av[0:N, N:384])
-    dinv[...] = rem1[0:N, 0:N]
-    invert(dinv, pbuf, qbuf)
-    e2[...] = dot(rem1[N:392, 0:N], dinv[...])
+    invert(dinv2, pbuf2, qbuf2)
+    e2[0:N, :] = dot(rem1[N:256, 0:N], dinv2[...])
+    dinv3[...] = rem1[N:256, N:256] - dot(e2[0:N, :], rem1[0:N, N:256])
+    e2[N:264, :] = dot(rem1[256:392, 0:N], dinv2[...])
+    rem2[...] = rem1[256:392, N:256] - dot(e2[N:264, :], rem1[0:N, N:256])
     snd[0:AUG, :] += dot_nt(e2[N:264, :], rem1[256:384, 0:N])
-    rem2[...] = rem1[N:392, N:256] - dot(e2[...], rem1[0:N, N:256])
-    dinv[...] = rem2[0:N, :]
-    invert(dinv, pbuf, qbuf)
-    h3[...] = dot(rem2[N:264, :], dinv[...])
-    snd[0:AUG, :] += dot_nt(h3[...], rem2[N:256, :])
+    invert(dinv3, pbuf, qbuf)
+    h3[...] = dot(rem2[...], dinv3[...])
+    snd[0:AUG, :] += dot_nt(h3[...], rem2[0:N, :])
     snd[AUG : AUG + 8, :] = wts[...]
 
     def y_copy(step, slot, part, src, sem):
@@ -248,6 +252,26 @@
     pass_b = y_copy(-1, 1, 1, recv_y.at[2], 5)
     for copy in (up_a, down_b, up_b, down_a):
         copy.start()
+
+    zt[:, 256:384] = h3[...]
+    zt[:, N:256] = e2[N:264, :] - dot(h3[...], e2[0:N, :])
+    zt[:, 0:N] = e1[256:392, :] - dot(zt[:, N:384], e1[0:256, :])
+
+    @pl.when(owner)
+    def _():
+        pltpu.make_async_remote_copy(
+            src_ref=gath.at[pl.ds(0, 63)], dst_ref=gath.at[pl.ds(0, 63)], send_sem=s_n.at[0],
+            recv_sem=r_n, device_id=dev(me + 1 - 2 * core), device_id_type=MESH,
+        ).wait_recv()
+        rhs = jnp.zeros((4, N), f32)
+        for i in range(64):
+            tile = gath[i]
+            nsys[2 * i : 2 * i + 2, :] = tile[0:2, :]
+            nlinks[2 * i : 2 * i + 2, :] = tile[2:4, :]
+            rhs = rhs + tile[4:8, :]
+        naug[0:N, :] = nlinks[...].T
+        nvec[...] = rhs
+
     other = 2 * y + 1 - core
     acc_m[...] = snd[0:AUG, :] * snd[pl.ds(AUG + mine, 1), :]
     acc_o[...] = snd[0:AUG, :] * snd[pl.ds(AUG + other, 1), :]
@@ -310,18 +334,7 @@
 
     @pl.when(owner)
     def _():
-        pltpu.make_async_remote_copy(
-            src_ref=gath.at[pl.ds(0, 63)], dst_ref=gath.at[pl.ds(0, 63)], send_sem=s_n.at[0],
-            recv_sem=r_n, device_id=dev(me + 1 - 2 * core), device_id_type=MESH,
-        ).wait_recv()
-        rhs = jnp.zeros((4, N), f32)
-        for i in range(64):
-            tile = gath[i]
-            nsys[2 * i : 2 * i + 2, :] = tile[0:2, :]
-            nlinks[2 * i : 2 * i + 2, :] = tile[2:4, :]
-            rhs = rhs + tile[4:8, :]
-        naug[0:N, :] = nlinks[...].T
-        acc_m[N : N + 4, :] += -rhs
+        acc_m[N : N + 4, :] += -nvec[...]
         acc_m[0:N, :] += nsys[...]
         for t in (1, 7, 2, 6, 3, 5, 4):
             source = (own_z + t) % 8
@@ -375,10 +388,6 @@
 
             lax.fori_loop(1 if far == 4 else 0, 8, send, 0)
         recv_n[mine] = msg[...]
-
-    zt[:, 256:384] = h3[...]
-    zt[:, N:256] = e2[N:264, :] - dot(h3[...], e2[0:N, :])
-    zt[:, 0:N] = e1[256:392, :] - dot(zt[:, N:384], e1[0:256, :])
 
     @pl.when(owner)
     def _():
@@ -457,11 +466,11 @@
         out_specs=vmem,
         scratch_shapes=[
             buf(384, 384), buf(384, N),
-            buf(AUG, 384), buf(N, N), buf(64, N), buf(64, N), buf(392, N), buf(392, 256), buf(264, N),
-            buf(264, N), buf(AUG, N), buf(8, N),
+            buf(AUG, 384), buf(N, N), buf(N, N), buf(N, N), buf(64, N), buf(64, N), buf(64, N), buf(64, N),
+            buf(392, N), buf(392, 256), buf(264, N), buf(AUG, N), buf(AUG, N), buf(8, N),
             buf(8, 8, N), buf(64, 8, N), buf(144, N), buf(3, 144, N), buf(AUG, N), buf(AUG, N),
             buf(AUG, N), buf(8, AUG, N),
-            buf(N, N), buf(N, N), buf(AUG, N), buf(AUG, N), buf(AUG, N), buf(8, 24, N),
+            buf(N, N), buf(4, N), buf(N, N), buf(AUG, N), buf(AUG, N), buf(AUG, N), buf(8, 24, N),
             buf(8, 24, N), buf(24, N), buf(8, 24, N), buf(24, N), buf(8, 24, N),
             buf(2, N), buf(8, 2, N), buf(AUG, 384), buf(8, N),
             dma((3,)), dma((8,)), dma, dma((6,)), dma((6,)), dma, dma, dma, dma((8,)),

time: 78.6 us -> 74.2 us (0.944)
  Pallas kernels: 77.1 us -> 72.7 us
    pallas_call x1, Pallas kernels: 75.9 us -> 71.4 us  [body(): pl.pallas_call(kernel, out_shape=jax.ShapeDtypeStruct((8, N), f32), in_sp...]
where the time goes in v3:
time: 74.2 us; the launch traced here: 74 us
  Pallas kernels  72.7 us (98%)
  between operations  1.29 us (2%)
    pallas_call x1, Pallas kernels, body(): pl.pallas_call(kernel, out_shape=jax.ShapeDtypeStruct((8, N), f32), in_sp...  71.4 us

profile of v3, /device:TPU:1, one launch (start us, length us, event | category | flops | bytes accessed | tf_op | source)
XLA Modules:
  0.0 74.0 jit_solution(5412353064179764518)
XLA Ops:
  1.3 71.4 %newton_step.1.packed = f32[8,128]{1,0:T(8,128)} custom-call(s32[1]{0:T(128)S(6)} %copy.12.parent, f32[1,384,384]{2,1,0:T(8,128)} %amat.1, f32[1,384,128]{2,1,0:T(8,128)} %coup.1, f32[1,384]{1,0:T(1,128)} %resid.1, f32[8,2,128]{2,1,0:T(2,128)} %nmat.1, f32[8,2,128]{2,1,0:T(2,128)} %nlink.1, f32[2,8]{1,0:T(2,128)} %bitcast.4, f32[128,128]{1,0:T(8,128)} %rmat.1, ...), custom_call_target="tpu_custom_call" | custom-call | tf_op jit(solution)/shard_map/newton_step/pallas_call | solution.py:459
  72.7 1.2 %unpack.1 = (f32[1,384]{1,0:T(1,128)}, f32[2,8]{1,0:T(2,128)}, f32[1,128]{1,0:T(1,128)}) custom-call(f32[8,128]{1,0:T(8,128)} %newton_step.1.packed), custom_call_target="tpu_custom_call" | custom-call | tf_op jit(solution)/shard_map/unpack/pallas_call | solution.py:485

commit v4 on v3

--- a/solution.py
+++ b/solution.py
@@ -12,6 +12,14 @@
 AUG = 136
 PANEL = 64
 GROUPS = PANEL // 8
+
+
+def rem(a, b):
+    return a % b if isinstance(a, int) else lax.rem(a, b)
+
+
+def div(a, b):
+    return a // b if isinstance(a, int) else lax.div(a, b)
 
 
 def dot(a, b):
@@ -127,8 +135,9 @@
 ):
     me = lax.axis_index("leaf")
     grp = lax.axis_index("grp")
-    y, z, core = me // 16, (me // 2) % 8, me % 2
-    own_z = 4 - grp // 4
+    y, z, core = div(me, 16), rem(div(me, 2), 8), rem(me, 2)
+    z_half = div(grp, 4)
+    own_z = 4 - z_half
     owner = z == own_z
     mine = 2 * y + core
 
@@ -136,7 +145,7 @@
         return {"leaf": leaf, "grp": grp}
 
     def owner_leaf(m, oz):
-        return (m // 2) * 16 + oz * 2 + m % 2
+        return div(m, 2) * 16 + oz * 2 + rem(m, 2)
 
     local = [
         pltpu.make_async_copy(amat.at[0, pl.ds(0, N), pl.ds(0, N)], dinv, s_l.at[0]),
@@ -148,19 +157,30 @@
 
     barrier = pltpu.get_barrier_semaphore()
 
-    def greet(t, carry):
-        pl.semaphore_signal(barrier, inc=1, device_id=dev((me + t) % 64), device_id_type=MESH)
-        return carry
-
-    lax.fori_loop(1, 64, greet, 0)
+    def greet(leaf):
+        pl.semaphore_signal(barrier, inc=1, device_id=dev(leaf), device_id_type=MESH)
+
+    @pl.when(jnp.logical_not(owner))
+    def _():
+        for step in (1, 3):
+            greet(rem(y + step, 4) * 16 + z * 2 + core)
+        greet(me + 1 - 2 * core)
+        for q in range(8):
+            greet(owner_leaf(q, own_z))
 
     @pl.when(owner)
     def _():
+        def greet_all(t, carry):
+            greet(rem(me + t, 64))
+            return carry
+
+        lax.fori_loop(1, 64, greet_all, 0)
+
         def greet_far(t, carry):
-            g = (grp + t) % 8
+            g = rem(grp + t, 8)
             pl.semaphore_signal(
                 barrier, inc=1,
-                device_id={"leaf": owner_leaf(mine, 4 - g // 4), "grp": g}, device_id_type=MESH,
+                device_id={"leaf": owner_leaf(mine, 4 - div(g, 4)), "grp": g}, device_id_type=MESH,
             )
             return carry
 
@@ -194,7 +214,7 @@
 
     @pl.when(jnp.logical_not(owner))
     def _():
-        pl.semaphore_wait(barrier, 63)
+        pl.semaphore_wait(barrier, 11)
 
     def node_copy(q, target):
         return pltpu.make_async_remote_copy(
@@ -243,7 +263,7 @@
         return pltpu.make_async_remote_copy(
             src_ref=src.at[rows], dst_ref=recv_y.at[slot, rows], send_sem=s_y.at[sem],
             recv_sem=r_y.at[2 * slot + part],
-            device_id=dev(((y + step + 4) % 4) * 16 + z * 2 + core), device_id_type=MESH,
+            device_id=dev(rem(y + step + 4, 4) * 16 + z * 2 + core), device_id_type=MESH,
         )
 
     up_a, up_b = y_copy(1, 0, 0, snd, 0), y_copy(1, 0, 1, snd, 1)
@@ -304,12 +324,12 @@
 
     def slice_copy(src, dst, send_sem, recv_sem, t, by_group):
         if by_group:
-            target = (grp + t) % 8
-            device = {"leaf": owner_leaf(mine, 4 - target // 4), "grp": target}
+            target = rem(grp + t, 8)
+            device = {"leaf": owner_leaf(mine, 4 - div(target, 4)), "grp": target}
             slot = grp
             source = src
         else:
-            target = (mine + t) % 8
+            target = rem(mine + t, 8)
             device = dev(owner_leaf(target, own_z))
             slot = mine
             source = src
@@ -325,11 +345,11 @@
         ).wait_recv()
 
     def message(far, t):
-        plane = far + (7 - 2 * far) * (grp // 4)
-        target = (mine + t) % 8
+        plane = far + (7 - 2 * far) * z_half
+        target = rem(mine + t, 8)
         return pltpu.make_async_remote_copy(
             src_ref=msg, dst_ref=recv_n.at[mine], send_sem=s_m.at[far, t], recv_sem=r_m.at[mine],
-            device_id=dev((target // 2) * 16 + plane * 2 + target % 2), device_id_type=MESH,
+            device_id=dev(div(target, 2) * 16 + plane * 2 + rem(target, 2)), device_id_type=MESH,
         )
 
     @pl.when(owner)
@@ -337,7 +357,7 @@
         acc_m[N : N + 4, :] += -nvec[...]
         acc_m[0:N, :] += nsys[...]
         for t in (1, 7, 2, 6, 3, 5, 4):
-            source = (own_z + t) % 8
+            source = rem(own_z + t, 8)
             z_copy(source).wait_recv()
             acc_m[...] += recv_z[source]
         dinv[...] = acc_m[0:N, :]
@@ -350,10 +370,10 @@
             send_r[q, 16:24, :] = rparts[N:AUG, :]
 
         for t in range(1, 8):
-            slice_copy(send_r.at[(mine + t) % 8], recv_r, s_r, r_r, t, False).start()
+            slice_copy(send_r.at[rem(mine + t, 8)], recv_r, s_r, r_r, t, False).start()
         recv_r[mine] = send_r[mine]
         for t in range(1, 8):
-            slot_wait(recv_r, s_r, r_r, (mine + t) % 8)
+            slot_wait(recv_r, s_r, r_r, rem(mine + t, 8))
         total = recv_r[0]
         for q in range(1, 8):
             total = total + recv_r[q]
@@ -362,7 +382,7 @@
             slice_copy(part, recv_g, s_g, r_g, t, True).start()
         recv_g[grp] = total
         for t in range(1, 8):
-            slot_wait(recv_g, s_g, r_g, (grp + t) % 8)
+            slot_wait(recv_g, s_g, r_g, rem(grp + t, 8))
         total = recv_g[0]
         for q in range(1, 8):
             total = total + recv_g[q]
@@ -371,7 +391,7 @@
             slice_copy(tot, recv_t, s_t, r_t, t, False).start()
         recv_t[mine] = total
         for t in range(1, 8):
-            slot_wait(recv_t, s_t, r_t, (mine + t) % 8)
+            slot_wait(recv_t, s_t, r_t, rem(mine + t, 8))
         for q in range(8):
             dinv[16 * q : 16 * q + 16, :] = rmat[16 * q : 16 * q + 16, :] + recv_t[q, 0:16, :]
         invert(dinv, pbuf, qbuf)
@@ -437,7 +457,7 @@
     @pl.when(owner)
     def _():
         for t in range(1, 8):
-            slice_copy(send_r.at[(mine + t) % 8], recv_r, s_r, r_r, t, False).wait_send()
+            slice_copy(send_r.at[rem(mine + t, 8)], recv_r, s_r, r_r, t, False).wait_send()
             slice_copy(part, recv_g, s_g, r_g, t, True).wait_send()
             slice_copy(tot, recv_t, s_t, r_t, t, False).wait_send()
 

time: 74.2 us -> 73 us (0.984)
  Pallas kernels: 72.7 us -> 71.5 us
    pallas_call x1, Pallas kernels: 71.4 us -> 70.2 us  [body(): pl.pallas_call(kernel, out_shape=jax.ShapeDtypeStruct((8, N), f32), in_sp...]
where the time goes in v4:
time: 73 us; the launch traced here: 72.8 us
  Pallas kernels  71.5 us (98%)
  between operations  1.29 us (2%)
    pallas_call x1, Pallas kernels, body(): pl.pallas_call(kernel, out_shape=jax.ShapeDtypeStruct((8, N), f32), in_sp...  70.2 us

profile of v4, /device:TPU:1, one launch (start us, length us, event | category | flops | bytes accessed | tf_op | source)
XLA Modules:
  0.0 72.8 jit_solution(7472253776787880272)
XLA Ops:
  1.3 70.2 %newton_step.1.packed = f32[8,128]{1,0:T(8,128)} custom-call(s32[1]{0:T(128)S(6)} %copy.12.parent, f32[1,384,384]{2,1,0:T(8,128)} %amat.1, f32[1,384,128]{2,1,0:T(8,128)} %coup.1, f32[1,384]{1,0:T(1,128)} %resid.1, f32[8,2,128]{2,1,0:T(2,128)} %nmat.1, f32[8,2,128]{2,1,0:T(2,128)} %nlink.1, f32[2,8]{1,0:T(2,128)} %bitcast.4, f32[128,128]{1,0:T(8,128)} %rmat.1, ...), custom_call_target="tpu_custom_call" | custom-call | tf_op jit(solution)/shard_map/newton_step/pallas_call | solution.py:479
  71.5 1.2 %unpack.1 = (f32[1,384]{1,0:T(1,128)}, f32[2,8]{1,0:T(2,128)}, f32[1,128]{1,0:T(1,128)}) custom-call(f32[8,128]{1,0:T(8,128)} %newton_step.1.packed), custom_call_target="tpu_custom_call" | custom-call | tf_op jit(solution)/shard_map/unpack/pallas_call | solution.py:505

commit v5 on v4

--- a/solution.py
+++ b/solution.py
@@ -137,7 +137,7 @@
     grp = lax.axis_index("grp")
     y, z, core = div(me, 16), rem(div(me, 2), 8), rem(me, 2)
     z_half = div(grp, 4)
-    own_z = 4 - z_half
+    own_z = 4 - 2 * z_half
     owner = z == own_z
     mine = 2 * y + core
 
@@ -180,7 +180,7 @@
             g = rem(grp + t, 8)
             pl.semaphore_signal(
                 barrier, inc=1,
-                device_id={"leaf": owner_leaf(mine, 4 - div(g, 4)), "grp": g}, device_id_type=MESH,
+                device_id={"leaf": owner_leaf(mine, 4 - 2 * div(g, 4)), "grp": g}, device_id_type=MESH,
             )
             return carry
 
@@ -325,7 +325,7 @@
     def slice_copy(src, dst, send_sem, recv_sem, t, by_group):
         if by_group:
             target = rem(grp + t, 8)
-            device = {"leaf": owner_leaf(mine, 4 - div(target, 4)), "grp": target}
+            device = {"leaf": owner_leaf(mine, 4 - 2 * div(target, 4)), "grp": target}
             slot = grp
             source = src
         else:
@@ -345,7 +345,7 @@
         ).wait_recv()
 
     def message(far, t):
-        plane = far + (7 - 2 * far) * z_half
+        plane = far + ((14 - far) % 8 - far) * z_half
         target = rem(mine + t, 8)
         return pltpu.make_async_remote_copy(
             src_ref=msg, dst_ref=recv_n.at[mine], send_sem=s_m.at[far, t], recv_sem=r_m.at[mine],
@@ -386,10 +386,10 @@
         total = recv_g[0]
         for q in range(1, 8):
             total = total + recv_g[q]
-        tot[...] = total
+        tot[...] = total[0:16, :]
         for t in range(1, 8):
             slice_copy(tot, recv_t, s_t, r_t, t, False).start()
-        recv_t[mine] = total
+        recv_t[mine] = total[0:16, :]
         for t in range(1, 8):
             slot_wait(recv_t, s_t, r_t, rem(mine + t, 8))
         for q in range(8):
@@ -491,7 +491,7 @@
             buf(8, 8, N), buf(64, 8, N), buf(144, N), buf(3, 144, N), buf(AUG, N), buf(AUG, N),
             buf(AUG, N), buf(8, AUG, N),
             buf(N, N), buf(4, N), buf(N, N), buf(AUG, N), buf(AUG, N), buf(AUG, N), buf(8, 24, N),
-            buf(8, 24, N), buf(24, N), buf(8, 24, N), buf(24, N), buf(8, 24, N),
+            buf(8, 24, N), buf(24, N), buf(8, 24, N), buf(16, N), buf(8, 16, N),
             buf(2, N), buf(8, 2, N), buf(AUG, 384), buf(8, N),
             dma((3,)), dma((8,)), dma, dma((6,)), dma((6,)), dma, dma, dma, dma((8,)),
             dma((8,)), dma((8,)), dma((8,)), dma((8,)), dma((8,)), dma((8,)), dma((8, 8)), dma((8,)),

time: 73 us -> 73.6 us (level)
  no operation moved by 1% of the time
where the time goes in v5:
time: 73.6 us; the launch traced here: 73.4 us
  Pallas kernels  72.1 us (98%)
  between operations  1.29 us (2%)
    pallas_call x1, Pallas kernels, body(): pl.pallas_call(kernel, out_shape=jax.ShapeDtypeStruct((8, N), f32), in_sp...  70.8 us

profile of v5, /device:TPU:1, one launch (start us, length us, event | category | flops | bytes accessed | tf_op | source)
XLA Modules:
  0.0 73.4 jit_solution(7657581697175468934)
XLA Ops:
  1.3 70.8 %newton_step.1.packed = f32[8,128]{1,0:T(8,128)} custom-call(s32[1]{0:T(128)S(6)} %copy.12.parent, f32[1,384,384]{2,1,0:T(8,128)} %amat.1, f32[1,384,128]{2,1,0:T(8,128)} %coup.1, f32[1,384]{1,0:T(1,128)} %resid.1, f32[8,2,128]{2,1,0:T(2,128)} %nmat.1, f32[8,2,128]{2,1,0:T(2,128)} %nlink.1, f32[2,8]{1,0:T(2,128)} %bitcast.4, f32[128,128]{1,0:T(8,128)} %rmat.1, ...), custom_call_target="tpu_custom_call" | custom-call | tf_op jit(solution)/shard_map/newton_step/pallas_call | solution.py:479
  72.1 1.2 %unpack.1 = (f32[1,384]{1,0:T(1,128)}, f32[2,8]{1,0:T(2,128)}, f32[1,128]{1,0:T(1,128)}) custom-call(f32[8,128]{1,0:T(8,128)} %newton_step.1.packed), custom_call_target="tpu_custom_call" | custom-call | tf_op jit(solution)/shard_map/unpack/pallas_call | solution.py:505
